TPU v7x, 32 devices: a whole 2x2x4 slice. The times are simulated.
32 devices in a mesh: dp: 8 (over z, x), tp: 4 (over y, core).
Axes of the slice: x: 2, y: 2, z: 4, core: 2. Of those that a mesh axis runs over, the one named last changes fastest.
Arguments:
- activations: bfloat16 [2048, 4096], P('dp'), may hold values from -6 to 6
- out_grads: bfloat16 [2048, 4096], P('dp', 'tp'), may hold values from -6 to 6
- residual: bfloat16 [32768, 4096], P('dp', 'tp'), may hold values from -24 to 24
- right_prev: bfloat16 [4096, 32], P('tp'), may hold values from -6 to 6
Outputs:
- update: bfloat16 [4096, 4096], P(None, 'tp')
- left_basis: float32 [4096, 32], replicated
- right_factor: float32 [4096, 32], P('tp')
All inputs are finite; a program needn't handle non-finite values.
Results may differ from a plain program's by a relative error of at most 0.0061.
Values sent between devices are 32-bit elements; how exact they have to be, the bound alone decides.
A program may use at most 64 MiB of HBM per device.

v0:
```python
import jax
import jax.numpy as jnp
from jax import lax
from jax.sharding import PartitionSpec as P


def shards(activations, out_grads, residual, right_prev):
    product = lax.dot_general(
        activations, out_grads, (((0,), (0,)), ((), ())), preferred_element_type=jnp.float32
    )
    merged = (product + residual.astype(jnp.float32)).astype(jnp.bfloat16)
    shard_sum = lax.psum_scatter(
        jnp.dot(merged, right_prev, preferred_element_type=jnp.float32),
        "tp",
        scatter_dimension=0,
        tiled=True,
    )
    block_sum = lax.psum(shard_sum, "dp")
    block_gram = jnp.dot(block_sum.T, block_sum, precision=lax.Precision.HIGHEST)
    gram_matrix = lax.psum(block_gram, "tp")
    lower_factor = jnp.linalg.cholesky(gram_matrix)
    basis_block = lax.linalg.triangular_solve(
        lower_factor, block_sum, left_side=False, lower=True, transpose_a=True
    )
    left_basis = lax.all_gather(basis_block, "tp", axis=0, tiled=True)
    left_half = left_basis.astype(jnp.bfloat16)
    coeff_terms = lax.dot_general(
        merged, left_half, (((0,), (0,)), ((), ())), preferred_element_type=jnp.float32
    )
    right_factor = lax.psum(coeff_terms, "dp") / lax.axis_size("dp")
    update = jnp.dot(left_basis, right_factor.T, precision=lax.Precision.HIGHEST).astype(
        jnp.bfloat16
    )
    return (update, left_basis, right_factor)


def solution(mesh):
    in_specs = (P("dp", None), P("dp", "tp"), P("dp", "tp"), P("tp", None))
    out_specs = (P(None, "tp"), P(), P("tp", None))
    return jax.shard_map(shards, mesh=mesh, in_specs=in_specs, out_specs=out_specs, check_vma=False)
```

profile of v0, /device:TPU:0, one launch (start us, length us, event | category | flops | bytes accessed | tf_op | source)
XLA Modules:
  0.0 244.7 jit_solution(3257671253548092697)
XLA Ops:
  7.2 0.0 copy-start
  7.2 0.0 copy-start.3
  7.2 0.0 reduce-scatter.2.cloned.1.call-start
  7.2 1.5 copy-done
  8.8 6.0 %add_convert_fusion = bf16[4096,1024]{1,0:T(8,128)(2,1)S(1)} fusion(bf16[4096,1024]{1,0:T(8,128)(2,1)} %param.6, bf16[256,4096]{1,0:T(8,128)(2,1)S(1)} %copy-done, bf16[256,1024]{1,0:T(8,128)(2,1)} %param.5), kind=kOutput, calls=%fused_computation | convolution fusion | flops 2160066560 | bytes 19398656 | tf_op jit(solution)/shard_map/dot_general | solution.py:8
  14.7 0.0 copy-start.1
  14.7 3.4 %copy-done.1 = bf16[4096,1024]{1,0:T(8,128)(2,1)} copy-done((bf16[4096,1024]{1,0:T(8,128)(2,1)}, bf16[4096,1024]{1,0:T(8,128)(2,1)S(1)}, u32[]{:S(2)}) %copy-start.1) | copy-done | bytes 8388632
  18.1 0.0 copy-done.3
  18.1 3.4 %fusion.6 = f32[4096,32]{0,1:T(8,128)} fusion(bf16[4096,1024]{1,0:T(8,128)(2,1)S(1)} %add_convert_fusion, bf16[1024,32]{0,1:T(8,128)(2,1)S(1)} %copy-done.3), kind=kOutput, calls=%fused_computation.15 | convolution fusion | flops 268435456 | bytes 8978432 | tf_op jit(solution)/shard_map/dot_general | solution.py:13
  21.5 0.0 reduce-scatter.2.cloned.1.call-update
  21.5 0.0 all-reduce.3.cloned.1.call-start
  21.6 24.5 %reduce-scatter.2.cloned.1.call-done = f32[1024,32]{0,1:T(8,128)} async-done(((f32[4096,32]{0,1:T(8,128)}), f32[1024,32]{0,1:T(8,128)}) %reduce-scatter.2.cloned.1.call-update) | async-done | bytes 131088 | tf_op jit(solution)/shard_map/reduce_scatter | solution.py:12
  46.0 0.0 all-reduce.3.cloned.1.call-update
  46.1 0.0 all-reduce.5.cloned.1.call-start
  46.1 73.8 %all-reduce.3.cloned.1.call-done = f32[1024,32]{0,1:T(8,128)} async-done(((f32[1024,32]{0,1:T(8,128)}), f32[1024,32]{0,1:T(8,128)}) %all-reduce.3.cloned.1.call-update) | async-done | bytes 131088 | tf_op jit(solution)/shard_map/psum | solution.py:18
  119.9 1.2 fusion.7
  121.1 10.1 %psum.22 = f32[32,32]{0,1:T(8,128)S(1)} all-reduce(f32[32,32]{0,1:T(8,128)S(1)} %fusion.7), channel_id=1, replica_groups=mesh['dp'=8,'tp'=4] {'tp'}, use_global_device_ids=true, to_apply=%region_2.0 | all-reduce | flops 1024 | bytes 8192 | tf_op jit(solution)/shard_map/psum | solution.py:20
  131.3 0.1 copy.8
  131.3 2.9 %cholesky.16 = f32[32,32]{1,0:T(8,128)S(1)} custom-call(f32[32,32]{1,0:T(8,128)S(1)} %fusion.5), custom_call_target="Cholesky" | custom-call | tf_op jit(solution)/shard_map/jit(cholesky)/cholesky | solution.py:21
  134.3 0.6 compare_reduce_fusion
  134.9 0.7 fusion.2
  135.6 2.4 custom-call.6
  138.0 1.2 fusion.3
  139.3 7.3 %all_gather.3 = f32[4096,32]{0,1:T(8,128)S(1)} all-gather(f32[1024,32]{0,1:T(8,128)S(1)} %fusion.3), channel_id=1, replica_groups=mesh['dp'=8,'tp'=4] {'tp'}, dimensions={0}, use_global_device_ids=true | all-gather | bytes 655360 | tf_op jit(solution)/shard_map/all_gather | solution.py:25
  146.6 5.6 %fusion = f32[1024,32]{0,1:T(8,128)} fusion(bf16[4096,1024]{1,0:T(8,128)(2,1)} %copy-done.1, f32[4096,32]{0,1:T(8,128)S(1)} %all_gather.3), kind=kOutput, calls=%fused_computation.2 | convolution fusion | flops 268566528 | bytes 9043968 | tf_op jit(solution)/shard_map/dot_general | solution.py:27
  152.1 0.0 all-reduce.5.cloned.1.call-update
  152.2 69.1 %all-reduce.5.cloned.1.call-done = f32[1024,32]{0,1:T(8,128)} async-done(((f32[1024,32]{0,1:T(8,128)}), f32[1024,32]{0,1:T(8,128)}) %all-reduce.5.cloned.1.call-update) | async-done | bytes 131088 | tf_op jit(solution)/shard_map/psum | solution.py:30
  221.2 0.9 broadcast_multiply_fusion
  222.1 0.0 copy-start.2
  222.1 15.3 %convolution_convert_fusion = bf16[4096,1024]{1,0:T(8,128)(2,1)} fusion(f32[4096,32]{0,1:T(8,128)S(1)} %all_gather.3, f32[1024,32]{0,1:T(8,128)S(1)} %broadcast_multiply_fusion), kind=kOutput, calls=%fused_computation.1 | convolution fusion | flops 1614807040 | bytes 9043968 | tf_op jit(solution)/shard_map/dot_general | solution.py:31
  237.4 0.8 copy.13
  238.2 0.0 copy-done.2
  (2 shorter events, 0.0 us)
Async XLA Ops:
  7.2 1.6 copy-start
  7.2 10.9 %copy-start.3 = (bf16[1024,32]{0,1:T(8,128)(2,1)S(1)}, bf16[1024,32]{0,1:T(8,128)(2,1)}, u32[]{:S(2)}) copy-start(bf16[1024,32]{0,1:T(8,128)(2,1)} %param.7) | copy-start | bytes 196612
  7.2 38.8 %reduce-scatter.2.cloned.1.call-start = ((), (), s32[]{:S(2)}) async-start(), calls=%async_computation.1 | async-start | bytes 655360 | tf_op jit(solution)/shard_map/reduce_scatter | solution.py:12
  14.7 3.4 %copy-start.1 = (bf16[4096,1024]{1,0:T(8,128)(2,1)}, bf16[4096,1024]{1,0:T(8,128)(2,1)S(1)}, u32[]{:S(2)}) copy-start(bf16[4096,1024]{1,0:T(8,128)(2,1)S(1)} %add_convert_fusion) | copy-start | bytes 25165828
  21.5 98.4 %all-reduce.3.cloned.1.call-start = ((), (), s32[]{:S(2)}) async-start(), calls=%async_computation.2 | async-start | bytes 262144 | tf_op jit(solution)/shard_map/psum | solution.py:18
  46.1 175.2 %all-reduce.5.cloned.1.call-start = ((), (), s32[]{:S(2)}) async-start(), calls=%async_computation.3 | async-start | bytes 262144 | tf_op jit(solution)/shard_map/psum | solution.py:30
  222.1 16.1 %copy-start.2 = (f32[1024,32]{0,1:T(8,128)}, f32[1024,32]{0,1:T(8,128)S(1)}, u32[]{:S(2)}) copy-start(f32[1024,32]{0,1:T(8,128)S(1)} %broadcast_multiply_fusion) | copy-start | bytes 393220
Sparse Core Ops, SparseCore 0:
  21.6 24.3 reduce-scatter.1
  49.4 70.4 all-reduce.2
  152.3 68.8 all-reduce.4
where the time goes:
time: 245 us
  waiting for transfers between devices  167 us (68%)
  matrix products  32.6 us (13%)
  blocking collectives  17.4 us (7%)
  between operations  13.8 us (6%)
  other arithmetic  7.6 us (3%)
  local copies, waits for them, and re-layouts  5.8 us (2%)
    psum x1, waiting for transfers between devices, shards(): block_sum = lax.psum(shard_sum, 'dp')  73.8 us
    psum x1, waiting for transfers between devices, shards(): right_factor = lax.psum(coeff_terms, 'dp') / lax.axis_size('dp')  69.1 us
    reduce_scatter x1, waiting for transfers between devices, shards(): lax.psum_scatter(jnp.dot(merged, right_prev, preferred_element_type=jnp.f...  24.5 us
    dot_general x1, matrix products, shards(): jnp.dot(left_basis, right_factor.T, precision=lax.Precision.HIGHEST)  15.3 us
    psum x1, blocking collectives, shards(): gram_matrix = lax.psum(block_gram, 'tp')  10.1 us
    all_gather x1, blocking collectives, shards(): left_basis = lax.all_gather(basis_block, 'tp', axis=0, tiled=True)  7.28 us
    dot_general x1, matrix products, shards(): lax.dot_general(activations, out_grads, (((0,), (0,)), ((), ())), preferr...  5.95 us
    unnamed x9, local copies, waits for them, and re-layouts  5.73 us
  transfers between devices with their start and end apart: 3, of which 3 were waited for; matrix products, arithmetic and copies ran while one was open for 0% of the time, Pallas kernels for 0%

commit v1 on v0

--- a/solution.py
+++ b/solution.py
@@ -15,7 +15,12 @@
         scatter_dimension=0,
         tiled=True,
     )
-    block_sum = lax.psum(shard_sum, "dp")
+    total_devices = jax.lax.axis_size("dp")
+    block_sum = shard_sum
+    for j in [at for at in (1, 2, 4, 8, 16) if at < total_devices]:
+        part_now = tuple(((hop_no, hop_no ^ j) for hop_no in range(total_devices)))
+        carry_in = jax.lax.ppermute(block_sum, "dp", part_now)
+        block_sum = block_sum + carry_in
     block_gram = jnp.dot(block_sum.T, block_sum, precision=lax.Precision.HIGHEST)
     gram_matrix = lax.psum(block_gram, "tp")
     lower_factor = jnp.linalg.cholesky(gram_matrix)

time: 245 us -> 190 us (0.78)
  waiting for transfers between devices: 167 us -> 108 us
  starting transfers between devices: 0.12 us -> 5.59 us
    psum x1 -> x0, waiting for transfers between devices: 73.8 us -> none  [shards(): block_sum = lax.psum(shard_sum, 'dp')]
    ppermute x0 -> x3, waiting for transfers between devices: none -> 12.1 us  [shards(): carry_in = jax.lax.ppermute(block_sum, 'dp', part_now)]
    ppermute x0 -> x3, starting transfers between devices: none -> 5.51 us  [shards(): carry_in = jax.lax.ppermute(block_sum, 'dp', part_now)]
  transfers between devices with their start and end apart: 3 -> 5, of which waited for: 3 -> 5; matrix products, arithmetic and copies ran while one was open for 0% -> 0% of each run, Pallas kernels for 0% -> 0%
where the time goes in v1:
time: 190 us; the launch traced here: 189 us
  waiting for transfers between devices  108 us (57%)
  matrix products  30.7 us (16%)
  blocking collectives  16.7 us (9%)
  between operations  14.1 us (7%)
  other arithmetic  8.56 us (5%)
  local copies, waits for them, and re-layouts  5.8 us (3%)
  starting transfers between devices  5.59 us (3%)
    psum x1, waiting for transfers between devices, shards(): right_factor = lax.psum(coeff_terms, 'dp') / lax.axis_size('dp')  71.3 us
    reduce_scatter x1, waiting for transfers between devices, shards(): lax.psum_scatter(jnp.dot(merged, right_prev, preferred_element_type=jnp.f...  24.5 us
    dot_general x1, matrix products, shards(): jnp.dot(left_basis, right_factor.T, precision=lax.Precision.HIGHEST)  15.3 us
    ppermute x3, waiting for transfers between devices, shards(): carry_in = jax.lax.ppermute(block_sum, 'dp', part_now)  12.1 us
    psum x1, blocking collectives, shards(): gram_matrix = lax.psum(block_gram, 'tp')  10.2 us
    all_gather x1, blocking collectives, shards(): left_basis = lax.all_gather(basis_block, 'tp', axis=0, tiled=True)  6.5 us
    dot_general x1, matrix products, shards(): lax.dot_general(activations, out_grads, (((0,), (0,)), ((), ())), preferr...  5.95 us
    unnamed x9, local copies, waits for them, and re-layouts  5.73 us
  transfers between devices with their start and end apart: 5, of which 5 were waited for; matrix products, arithmetic and copies ran while one was open for 0% of the time, Pallas kernels for 0%

profile of v1, /device:TPU:0, one launch (start us, length us, event | category | flops | bytes accessed | tf_op | source)
XLA Modules:
  0.0 189.5 jit_solution(7611215638912217870)
XLA Ops:
  7.2 0.0 copy-start
  7.2 0.0 copy-start.3
  7.2 0.0 reduce-scatter.2.cloned.1.call-start
  7.2 1.5 copy-done
  8.8 6.0 %add_convert_fusion = bf16[4096,1024]{1,0:T(8,128)(2,1)S(1)} fusion(bf16[4096,1024]{1,0:T(8,128)(2,1)} %param.6, bf16[256,4096]{1,0:T(8,128)(2,1)S(1)} %copy-done, bf16[256,1024]{1,0:T(8,128)(2,1)} %param.5), kind=kOutput, calls=%fused_computation | convolution fusion | flops 2160066560 | bytes 19398656 | tf_op jit(solution)/shard_map/dot_general | solution.py:8
  14.7 0.0 copy-start.1
  14.7 3.4 %copy-done.1 = bf16[4096,1024]{1,0:T(8,128)(2,1)} copy-done((bf16[4096,1024]{1,0:T(8,128)(2,1)}, bf16[4096,1024]{1,0:T(8,128)(2,1)S(1)}, u32[]{:S(2)}) %copy-start.1) | copy-done | bytes 8388632
  18.1 0.0 copy-done.3
  18.1 3.4 %fusion.6 = f32[4096,32]{0,1:T(8,128)} fusion(bf16[4096,1024]{1,0:T(8,128)(2,1)S(1)} %add_convert_fusion, bf16[1024,32]{0,1:T(8,128)(2,1)S(1)} %copy-done.3), kind=kOutput, calls=%fused_computation.15 | convolution fusion | flops 268435456 | bytes 8978432 | tf_op jit(solution)/shard_map/dot_general | solution.py:13
  21.5 0.0 reduce-scatter.2.cloned.1.call-update
  21.5 0.0 all-reduce.2.cloned.1.call-start
  21.6 24.5 %reduce-scatter.2.cloned.1.call-done = f32[1024,32]{0,1:T(8,128)} async-done(((f32[4096,32]{0,1:T(8,128)}), f32[1024,32]{0,1:T(8,128)}) %reduce-scatter.2.cloned.1.call-update) | async-done | bytes 131088 | tf_op jit(solution)/shard_map/reduce_scatter | solution.py:12
  46.0 1.5 collective-permute-start
  47.5 3.8 %collective-permute-done = f32[1024,32]{0,1:T(8,128)S(1)} collective-permute-done((f32[1024,32]{0,1:T(8,128)}, f32[1024,32]{0,1:T(8,128)S(1)}, u32[]{:S(2)}, u32[]{:S(2)}) %collective-permute-start) | collective-permute-done | bytes 131104 | tf_op jit(solution)/shard_map/ppermute | solution.py:22
  51.3 0.9 add.30
  52.2 1.6 collective-permute-start.1
  53.8 3.5 %collective-permute-done.1 = f32[1024,32]{0,1:T(8,128)S(1)} collective-permute-done((f32[1024,32]{0,1:T(8,128)S(1)}, f32[1024,32]{0,1:T(8,128)S(1)}, u32[]{:S(2)}, u32[]{:S(2)}) %collective-permute-start.1) | collective-permute-done | bytes 131104 | tf_op jit(solution)/shard_map/ppermute | solution.py:22
  57.3 2.5 %collective-permute-start.2 = (f32[1024,32]{0,1:T(8,128)S(1)}, f32[1024,32]{0,1:T(8,128)S(1)}, u32[]{:S(2)}, u32[]{:S(2)}) collective-permute-start(f32[1024,32]{0,1:T(8,128)S(1)} %add.31), channel_id=1, source_target_pairs={{0,16},{4,20},{8,24},{12,28},{16,0},{20,4},{24,8},{28,12},{1,17},{... | collective-permute-start | bytes 393224 | tf_op jit(solution)/shard_map/ppermute | solution.py:22
  59.8 4.8 %collective-permute-done.2 = f32[1024,32]{0,1:T(8,128)S(1)} collective-permute-done((f32[1024,32]{0,1:T(8,128)S(1)}, f32[1024,32]{0,1:T(8,128)S(1)}, u32[]{:S(2)}, u32[]{:S(2)}) %collective-permute-start.2) | collective-permute-done | bytes 131104 | tf_op jit(solution)/shard_map/ppermute | solution.py:22
  64.6 0.2 fusion.7
  64.9 10.2 %psum.14 = f32[32,32]{0,1:T(8,128)S(1)} all-reduce(f32[32,32]{0,1:T(8,128)S(1)} %fusion.7), channel_id=1, replica_groups=mesh['dp'=8,'tp'=4] {'tp'}, use_global_device_ids=true, to_apply=%region_1.0 | all-reduce | flops 1024 | bytes 8192 | tf_op jit(solution)/shard_map/psum | solution.py:25
  75.1 0.1 copy.8
  75.2 2.9 %cholesky.16 = f32[32,32]{1,0:T(8,128)S(1)} custom-call(f32[32,32]{1,0:T(8,128)S(1)} %fusion.5), custom_call_target="Cholesky" | custom-call | tf_op jit(solution)/shard_map/jit(cholesky)/cholesky | solution.py:26
  78.2 0.6 compare_reduce_fusion
  78.8 0.7 fusion.2
  79.5 2.4 %custom-call.6 = f32[1,32,32]{1,2,0:T(8,128)S(1)} custom-call(f32[1,32,32]{2,1,0:T(8,128)S(1)} %fusion.2), custom_call_target="InvertDiagBlocksLowerTriangular" | custom-call | tf_op jit(solution)/shard_map/triangular_solve | solution.py:27
  81.9 0.3 fusion.3
  82.2 6.5 %all_gather.3 = f32[4096,32]{0,1:T(8,128)S(1)} all-gather(f32[1024,32]{0,1:T(8,128)S(1)} %fusion.3), channel_id=1, replica_groups=mesh['dp'=8,'tp'=4] {'tp'}, dimensions={0}, use_global_device_ids=true | all-gather | bytes 655360 | tf_op jit(solution)/shard_map/all_gather | solution.py:30
  88.8 5.6 %fusion = f32[1024,32]{0,1:T(8,128)} fusion(bf16[4096,1024]{1,0:T(8,128)(2,1)} %copy-done.1, f32[4096,32]{0,1:T(8,128)S(1)} %all_gather.3), kind=kOutput, calls=%fused_computation.2 | convolution fusion | flops 268566528 | bytes 9043968 | tf_op jit(solution)/shard_map/dot_general | solution.py:32
  94.3 0.0 all-reduce.2.cloned.1.call-update
  94.4 71.3 %all-reduce.2.cloned.1.call-done = f32[1024,32]{0,1:T(8,128)} async-done(((f32[1024,32]{0,1:T(8,128)}), f32[1024,32]{0,1:T(8,128)}) %all-reduce.2.cloned.1.call-update) | async-done | bytes 131088 | tf_op jit(solution)/shard_map/psum | solution.py:35
  165.6 0.9 broadcast_multiply_fusion
  166.5 0.0 copy-start.2
  166.6 15.3 %convolution_convert_fusion = bf16[4096,1024]{1,0:T(8,128)(2,1)} fusion(f32[4096,32]{0,1:T(8,128)S(1)} %all_gather.3, f32[1024,32]{0,1:T(8,128)S(1)} %broadcast_multiply_fusion), kind=kOutput, calls=%fused_computation.1 | convolution fusion | flops 1614807040 | bytes 9043968 | tf_op jit(solution)/shard_map/dot_general | solution.py:36
  181.8 0.8 copy.12
  182.6 0.0 copy-done.2
  (4 shorter events, 0.1 us)
Async XLA Ops:
  7.2 1.6 copy-start
  7.2 10.9 %copy-start.3 = (bf16[1024,32]{0,1:T(8,128)(2,1)S(1)}, bf16[1024,32]{0,1:T(8,128)(2,1)}, u32[]{:S(2)}) copy-start(bf16[1024,32]{0,1:T(8,128)(2,1)} %param.7) | copy-start | bytes 196612
  7.2 38.8 %reduce-scatter.2.cloned.1.call-start = ((), (), s32[]{:S(2)}) async-start(), calls=%async_computation.1 | async-start | bytes 655360 | tf_op jit(solution)/shard_map/reduce_scatter | solution.py:12
  14.7 3.4 %copy-start.1 = (bf16[4096,1024]{1,0:T(8,128)(2,1)}, bf16[4096,1024]{1,0:T(8,128)(2,1)S(1)}, u32[]{:S(2)}) copy-start(bf16[4096,1024]{1,0:T(8,128)(2,1)S(1)} %add_convert_fusion) | copy-start | bytes 25165828
  21.5 144.1 %all-reduce.2.cloned.1.call-start = ((), (), s32[]{:S(2)}) async-start(), calls=%async_computation.2 | async-start | bytes 262144 | tf_op jit(solution)/shard_map/psum | solution.py:35
  46.0 5.3 %collective-permute-start = (f32[1024,32]{0,1:T(8,128)}, f32[1024,32]{0,1:T(8,128)S(1)}, u32[]{:S(2)}, u32[]{:S(2)}) collective-permute-start(f32[1024,32]{0,1:T(8,128)} %reduce-scatter.2.cloned.1.call-done), channel_id=1, source_target_pairs={{0,4},{4,0},{8,12},{12,8},{16,20},{20,16},{24,28},{28,24},{1,5},{5... | collective-permute-start | bytes 393224 | tf_op jit(solution)/shard_map/ppermute | solution.py:22
  52.2 5.0 %collective-permute-start.1 = (f32[1024,32]{0,1:T(8,128)S(1)}, f32[1024,32]{0,1:T(8,128)S(1)}, u32[]{:S(2)}, u32[]{:S(2)}) collective-permute-start(f32[1024,32]{0,1:T(8,128)S(1)} %add.30), channel_id=1, source_target_pairs={{0,8},{4,12},{8,0},{12,4},{16,24},{20,28},{24,16},{28,20},{1,9},{5... | collective-permute-start | bytes 393224 | tf_op jit(solution)/shard_map/ppermute | solution.py:22
  57.3 7.3 %collective-permute-start.2 = (f32[1024,32]{0,1:T(8,128)S(1)}, f32[1024,32]{0,1:T(8,128)S(1)}, u32[]{:S(2)}, u32[]{:S(2)}) collective-permute-start(f32[1024,32]{0,1:T(8,128)S(1)} %add.31), channel_id=1, source_target_pairs={{0,16},{4,20},{8,24},{12,28},{16,0},{20,4},{24,8},{28,12},{1,17},{... | collective-permute-start | bytes 393224 | tf_op jit(solution)/shard_map/ppermute | solution.py:22
  166.5 16.1 %copy-start.2 = (f32[1024,32]{0,1:T(8,128)}, f32[1024,32]{0,1:T(8,128)S(1)}, u32[]{:S(2)}) copy-start(f32[1024,32]{0,1:T(8,128)S(1)} %broadcast_multiply_fusion) | copy-start | bytes 393220
Sparse Core Ops, SparseCore 0:
  21.6 24.3 reduce-scatter.1
  94.5 71.1 all-reduce.1
